TPU v7x, 128 devices: a whole 4x4x4 slice. The times are simulated.
128 devices in a mesh: grp: 4 (over y), dom: 32 (over z, x, core).
Axes of the slice: x: 4, y: 4, z: 4, core: 2. Of those that a mesh axis runs over, the one named last changes fastest.
Arguments:
- fields: float32 [210, 131072], P(None, ('grp', 'dom')), may hold values from -6 to 6
- metric: float32 [9, 131072], P(None, ('grp', 'dom')), may hold values from -5 to 5
- normals: float32 [12, 131072], P(None, ('grp', 'dom')), may hold values from -3 to 3
- fscale: float32 [4, 131072], P(None, ('grp', 'dom')), may hold values from 0.5 to 4
- orders: int32 [131072], P(('grp', 'dom')), may hold values from 1 to 4, as said below
- slots: int32 [131072], P(('grp', 'dom')), may hold values from 0 to 511, as said below
- send_faces: int32 [1179648], P(('grp', 'dom')), may hold values from 0 to 8192, as said below
- recv_faces: int32 [1048576], P(('grp', 'dom')), may hold values from 0 to 9216, as said below
- dmat: float32 [4, 105, 35], P('grp'), may hold values from -4 to 4
- tmat: float32 [4, 60, 35], P('grp'), may hold values from -4 to 4
- lmat: float32 [4, 35, 60], P('grp'), may hold values from -3 to 3
Outputs:
- rhs: float32 [210, 262144], P(None, ('grp', 'dom'))
Inputs may be any that keep to these rules, and one draw needn't show every extreme that they name: `orders`: on each device every order from 1 to 4 is held by at least one element and by at most 512; one order is held by exactly 512. The elements of one device that share an order have distinct slots. `send_faces`: each entry names a face of an occupied slot of the sending bucket or equals 4 * 2048 (nothing); in each list the items in use stand first. `recv_faces`: every face of an occupied slot names a distinct received item that is in use, and every item in use is named by exactly one face; faces of empty slots hold 9216. A list carries at most 768 items in use, and some list carries exactly 768.
All inputs are finite; a program needn't handle non-finite values.
Results may differ from a plain program's by a relative error of at most 0.0003.
Values sent between devices are 32-bit elements; how exact they have to be, the bound alone decides.
No kernel may reach another device: no remote copies, remote signals or barrier semaphores. Data moves between devices by JAX's collectives and lax.ppermute only.
A program may use at most 128 MiB of HBM per device.

v0:
```python
import jax
import jax.numpy as jnp
from jax import lax
from jax.sharding import PartitionSpec as P

NPM = 35
FPTS = 15


exact_prec = lax.Precision.HIGHEST


def shifted(x, axis, by):
    size = lax.axis_size(axis)
    return lax.ppermute(x, axis, [(i, (i + by) % size) for i in range(size)])


def order_mask(order_index):
    node_total = (order_index + 2) * (order_index + 3) * (order_index + 4) // 6
    return (jnp.arange(NPM, dtype=jnp.int32) < node_total).astype(jnp.float32)


def cross_of(first_vec, second_vec):
    return [
        first_vec[1] * second_vec[2] - first_vec[2] * second_vec[1],
        first_vec[2] * second_vec[0] - first_vec[0] * second_vec[2],
        first_vec[0] * second_vec[1] - first_vec[1] * second_vec[0],
    ]


def volume_terms(coefficients, metric_cols, deriv_mats):
    derived = jnp.einsum("anm,qms->qans", deriv_mats, coefficients, precision=exact_prec)

    def partial_of(component, direction):
        return (
            metric_cols[0, direction][None] * derived[component, 0]
            + metric_cols[1, direction][None] * derived[component, 1]
            + metric_cols[2, direction][None] * derived[component, 2]
        )

    curl_h = [
        partial_of(5, 1) - partial_of(4, 2),
        partial_of(3, 2) - partial_of(5, 0),
        partial_of(4, 0) - partial_of(3, 1),
    ]
    curl_e = [
        partial_of(2, 1) - partial_of(1, 2),
        partial_of(0, 2) - partial_of(2, 0),
        partial_of(1, 0) - partial_of(0, 1),
    ]
    return jnp.stack(curl_h + [-value for value in curl_e], 0)


def face_flux(own_traces, neighbour, normal_cols, scale_cols):
    own_split = own_traces.reshape(6, FPTS, -1)
    far_split = neighbour.reshape(6, FPTS, -1)
    jump_e = [far_split[c] - own_split[c] for c in range(3)]
    jump_h = [far_split[c + 3] - own_split[c + 3] for c in range(3)]
    normal = [normal_cols[c] for c in range(3)]
    normal_e = normal[0] * jump_e[0] + normal[1] * jump_e[1] + normal[2] * jump_e[2]
    normal_h = normal[0] * jump_h[0] + normal[1] * jump_h[1] + normal[2] * jump_h[2]
    turn_h = cross_of(normal, jump_h)
    turn_e = cross_of(normal, jump_e)
    flux_e = [0.5 * scale_cols * (turn_h[c] + jump_e[c] - normal[c] * normal_e) for c in range(3)]
    flux_h = [0.5 * scale_cols * (-turn_e[c] + jump_h[c] - normal[c] * normal_h) for c in range(3)]
    return jnp.stack(flux_e + flux_h, 0)


def block_rhs(bucket, own_traces, neighbour, deriv_mats, lift_mat):
    slot_count = bucket.shape[1]
    coefficients = bucket[: 6 * NPM].reshape(6, NPM, slot_count)
    metric_cols = bucket[6 * NPM : 6 * NPM + 9].reshape(3, 3, slot_count)
    normal_cols = bucket[6 * NPM + 9 : 6 * NPM + 21].reshape(3, 1, 4 * slot_count)
    scale_cols = bucket[6 * NPM + 21 : 6 * NPM + 25].reshape(1, 4 * slot_count)
    volume = volume_terms(coefficients, metric_cols, deriv_mats)
    flux = face_flux(own_traces, neighbour, normal_cols, scale_cols).reshape(
        6, FPTS * 4, slot_count
    )
    lifted = jnp.einsum("mp,qps->qms", lift_mat, flux, precision=exact_prec)
    return (volume + lifted).reshape(6 * NPM, slot_count)


def across_groups(outgoing):
    return lax.all_to_all(outgoing, "grp", split_axis=1, concat_axis=1, tiled=True)


def across_columns(outgoing):
    lowered = shifted(outgoing[0], "dom", -1)
    raised = shifted(outgoing[2], "dom", 1)
    return jnp.stack([lowered, outgoing[1], raised], 0)


def local(fields, metric, normals, fscale, orders, slots, send_faces, recv_faces, dmat, tmat, lmat):
    own_group = lax.axis_index("grp")
    groups = lax.axis_size("grp")
    elements = fields.shape[1]
    capacity = elements // 2
    slot_count = groups * capacity
    payload = jnp.concatenate([fields, metric, normals, fscale], 0)
    row_count = payload.shape[0]
    zero_column = jnp.zeros((row_count, 1), jnp.float32)
    target = (orders - 1) * capacity + slots
    inverse = (
        jnp.full((slot_count,), elements, jnp.int32)
        .at[target]
        .set(jnp.arange(elements, dtype=jnp.int32))
    )
    padded = jnp.concatenate([payload, zero_column], 1)
    outgoing = jnp.take(padded, inverse, axis=1).reshape(row_count, groups, capacity)
    bucket = lax.all_to_all(outgoing, "grp", split_axis=1, concat_axis=1, tiled=True).reshape(
        row_count, slot_count
    )
    node_mask = order_mask(own_group)
    deriv_mats = dmat[0].reshape(3, NPM, NPM) * node_mask[None, :, None] * node_mask[None, None, :]
    trace_mat = tmat[0] * node_mask[None, :]
    lift_mat = lmat[0] * node_mask[:, None]
    coefficients = bucket[: 6 * NPM].reshape(6, NPM, slot_count)
    own_traces = jnp.einsum("pm,qms->qps", trace_mat, coefficients, precision=exact_prec).reshape(
        6 * FPTS, 4 * slot_count
    )
    face_rows = jnp.concatenate([own_traces.T, jnp.zeros((1, 6 * FPTS), jnp.float32)], 0)
    list_total = send_faces.shape[0]
    list_size = list_total // (3 * groups)
    outgoing_faces = jnp.take(face_rows, send_faces, axis=0).reshape(3, groups, list_size, 6 * FPTS)
    arrived = across_columns(across_groups(outgoing_faces))
    received = jnp.concatenate(
        [arrived.reshape(list_total, 6 * FPTS), jnp.zeros((1, 6 * FPTS), jnp.float32)], 0
    )
    neighbour = jnp.take(received, recv_faces, axis=0).T
    return block_rhs(bucket, own_traces, neighbour, deriv_mats, lift_mat)


def solution(mesh):
    in_specs = (
        P(None, ("grp", "dom")),
        P(None, ("grp", "dom")),
        P(None, ("grp", "dom")),
        P(None, ("grp", "dom")),
        P(("grp", "dom")),
        P(("grp", "dom")),
        P(("grp", "dom")),
        P(("grp", "dom")),
        P("grp", None, None),
        P("grp", None, None),
        P("grp", None, None),
    )
    out_specs = P(None, ("grp", "dom"))
    return jax.shard_map(local, mesh=mesh, in_specs=in_specs, out_specs=out_specs, check_vma=False)
```

profile of v0, /device:TPU:39, one launch (start us, length us, event | category | flops | bytes accessed | tf_op | source)
XLA Modules:
  0.0 278.0 jit_solution(4763983993886906199)
XLA Ops:
  0.7 4.3 %scatter_custom_fusion = s32[2048]{0:T(1024)S(1)} fusion(s32[1024]{0:T(1024)S(1)} %compare_select_fusion.3, s32[1024]{0:T(1024)S(1)} %iota.14, s32[]{:T(128)} %constant.33.clone.1), kind=kCustom, calls=%fused_computation.79 | custom fusion | bytes 8196 | tf_op jit(solution)/shard_map/scatter | solution.py:106
  11.3 6.6 %gather_fusion = f32[2048,235]{1,0:T(8,128)S(1)} fusion(f32[235,1025]{0,1:T(8,128)S(1)} %select_maximum_fusion, s32[2048]{0:T(1024)S(1)} %fusion.11), kind=kCustom, calls=%fused_computation | custom fusion | bytes 3858432 | tf_op jit(solution)/shard_map/jit(_take)/gather | solution.py:109
  19.8 3.1 %broadcast_select_fusion.1 = f32[235,4,512]{2,0,1:T(8,128)} fusion(f32[235,4,512]{2,0,1:T(8,128)} %copy.62, pred[4,512]{1,0:T(4,128)(4,1)S(1)} %broadcast_in_dim.53), kind=kLoop, calls=%fused_computation.20 | loop fusion | flops 481280 | bytes 3852288 | tf_op jit(solution)/shard_map/jit(_take)/select_n | solution.py:109
  22.9 4.8 %all-to-all-start = ((f32[235,4,512]{2,0,1:T(8,128)}), f32[235,4,512]{2,0,1:T(8,128)S(1)}, u32[]{:S(2)}, u32[]{:S(2)}) async-start(f32[235,4,512]{2,0,1:T(8,128)} %broadcast_select_fusion.1), calls=%async_computation | async-start | bytes 3932160 | tf_op jit(solution)/shard_map/all_to_all | solution.py:110
  30.3 21.5 %all-to-all-done = f32[235,4,512]{2,0,1:T(8,128)S(1)} async-done(((f32[235,4,512]{2,0,1:T(8,128)}), f32[235,4,512]{2,0,1:T(8,128)S(1)}, u32[]{:S(2)}, u32[]{:S(2)}) %all-to-all-start) | async-done | bytes 1925152 | tf_op jit(solution)/shard_map/all_to_all | solution.py:110
  54.4 2.5 reshape.2020
  56.9 2.6 reshape.2060
  59.4 4.7 %convolution_bitcast_fusion.1 = f32[6,60,2048]{2,1,0:T(8,128)S(1)} fusion(f32[6,35,2048]{2,1,0:T(8,128)} %reshape.2020, f32[1,60,35]{1,0,2:T(1,128)S(1)} %broadcast_multiply_fusion), kind=kOutput, calls=%fused_computation.7 | convolution fusion | flops 309657600 | bytes 4677840 | tf_op jit(solution)/shard_map/pm,qms->qps/dot_general | solution.py:118
  64.1 3.0 %reshape.2021 = f32[90,8192]{1,0:T(8,128)} reshape(f32[6,60,2048]{2,1,0:T(8,128)S(1)} %convolution_bitcast_fusion.1) | data formatting | bytes 5898240 | tf_op jit(solution)/shard_map/reshape | solution.py:118
  67.1 5.2 %copy.67 = f32[90,8192]{0,1:T(8,128)} copy(f32[90,8192]{1,0:T(8,128)} %reshape.2021) | data formatting | bytes 5898240 | tf_op jit(solution)/shard_map/reshape | solution.py:118
  72.3 3.8 %concatenate.15 = f32[8193,90]{1,0:T(8,128)} pad(f32[8192,90]{1,0:T(8,128)} %bitcast.170, f32[]{:T(128)} %constant.45.clone.1), padding=0_1x0_0 | pad | bytes 5898604 | tf_op jit(solution)/shard_map/concatenate | solution.py:121
  76.0 33.3 %gather_fusion.1 = f32[9216,90]{1,0:T(8,128)} fusion(f32[8193,90]{1,0:T(8,128)} %concatenate.15, s32[9216]{0:T(1024)S(1)} %fusion.3), kind=kCustom, calls=%fused_computation.1 | custom fusion | bytes 6672384 | tf_op jit(solution)/shard_map/jit(_take)/gather | solution.py:124
  109.4 3.9 %copy.68 = f32[3,4,768,90]{2,3,0,1:T(8,128)S(1)} copy(f32[3,4,768,90]{3,2,1,0:T(8,128)} %bitcast.168) | data formatting | bytes 6635520 | tf_op jit(solution)/shard_map/jit(_take)/gather | solution.py:124
  115.5 3.9 %all-to-all-start.1 = ((f32[3,4,768,90]{2,3,0,1:T(8,128)}), f32[3,4,768,90]{2,3,0,1:T(8,128)S(1)}, u32[]{:S(2)}, u32[]{:S(2)}) async-start(f32[3,4,768,90]{2,3,0,1:T(8,128)} %broadcast_select_fusion), calls=%async_computation.1 | async-start | bytes 7077888 | tf_op jit(solution)/shard_map/all_to_all | solution.py:84
  119.4 10.5 %convolution_bitcast_fusion = f32[6,3,35,2048]{3,2,1,0:T(8,128)} fusion(f32[6,35,2048,1]{2,1,0,3:T(8,128)} %reshape.2060, f32[3,35,35]{2,1,0:T(8,128)} %copy.65), kind=kOutput, calls=%fused_computation.5 | convolution fusion | flops 541900800 | bytes 6895980 | tf_op jit(solution)/shard_map/anm,qms->qans/dot_general | solution.py:32
  143.8 15.6 %all-to-all-done.1 = f32[3,4,768,90]{2,3,0,1:T(8,128)S(1)} async-done(((f32[3,4,768,90]{2,3,0,1:T(8,128)}), f32[3,4,768,90]{2,3,0,1:T(8,128)S(1)}, u32[]{:S(2)}, u32[]{:S(2)}) %all-to-all-start.1) | async-done | bytes 3317792 | tf_op jit(solution)/shard_map/all_to_all | solution.py:84
  161.4 4.2 %collective-permute-start.1 = (f32[4,768,90]{1,0,2:T(4,128)S(1)}, f32[4,768,90]{1,0,2:T(4,128)S(1)}, u32[]{:S(2)}, u32[]{:S(2)}) collective-permute-start(f32[4,768,90]{1,0,2:T(4,128)S(1)} %copy.71), channel_id=1, source_target_pairs={{0,1},{1,2},{2,3},{3,4},{4,5},{5,6},{6,7},{7,8},{8,9},{9,10},{10,1... | collective-permute-start | bytes 3317768 | tf_op jit(solution)/shard_map/ppermute | solution.py:15
  175.4 2.4 negate_dynamic-update-slice_fusion
  178.1 6.6 %collective-permute-done = f32[4,768,90]{1,0,2:T(4,128)} collective-permute-done((f32[4,768,90]{1,0,2:T(4,128)}, f32[4,768,90]{1,0,2:T(4,128)}, u32[]{:S(2)}, u32[]{:S(2)}) %collective-permute-start) | collective-permute-done | bytes 1105952 | tf_op jit(solution)/shard_map/ppermute | solution.py:15
  186.5 3.6 %copy.73 = f32[3,4,768,90]{3,2,1,0:T(8,128)} copy(f32[3,4,768,90]{2,3,0,1:T(8,128)S(1)} %pad_maximum_fusion) | data formatting | bytes 6635520 | tf_op jit(solution)/shard_map/stack | solution.py:90
  190.1 4.0 %concatenate.16 = f32[9217,90]{1,0:T(8,128)} pad(f32[9216,90]{1,0:T(8,128)} %bitcast.169, f32[]{:T(128)} %constant.45.clone.1), padding=0_1x0_0 | pad | bytes 6635884 | tf_op jit(solution)/shard_map/concatenate | solution.py:126
  194.0 30.1 %gather_fusion.2 = f32[8192,90]{1,0:T(8,128)} fusion(f32[9217,90]{1,0:T(8,128)} %concatenate.16, s32[8192]{0:T(1024)S(1)} %copy-done.25), kind=kCustom, calls=%fused_computation.2 | custom fusion | bytes 5931008 | tf_op jit(solution)/shard_map/jit(_take)/gather | solution.py:129
  224.1 6.2 %select_bitcast_fusion = f32[90,8192]{0,1:T(8,128)S(1)} fusion(f32[8192,90]{1,0:T(8,128)} %gather_fusion.2, pred[8192]{0:T(1024)(128)(4,1)S(1)} %copy-done.26), kind=kLoop, calls=%fused_computation.4 | loop fusion | flops 737280 | bytes 5906432 | tf_op jit(solution)/shard_map/jit(_take)/select_n | solution.py:129
  230.4 11.1 %fusion.14 = (f32[15,8192]{0,1:T(8,128)}, f32[15,8192]{0,1:T(8,128)}, f32[15,8192]{0,1:T(8,128)}, f32[15,8192]{0,1:T(8,128)}, f32[15,8192]{0,1:T(8,128)}, /*index=5*/f32[15,8192]{0,1:T(8,128)}) fusion(f32[90,8192]{0,1:T(8,128)S(1)} %select_bitcast_fusion), kind=kLoop, calls=%fused_computation.82 | loop fusion | bytes 5898240 | tf_op jit(solution)/shard_map/slice | solution.py:58
  241.4 2.8 %copy.74 = f32[15,8192]{1,0:T(8,128)S(1)} copy(f32[15,8192]{0,1:T(8,128)} %get-tuple-element.18) | data formatting | bytes 983040 | tf_op jit(solution)/shard_map/slice | solution.py:58
  245.2 2.8 %copy.75 = f32[15,8192]{1,0:T(8,128)S(1)} copy(f32[15,8192]{0,1:T(8,128)} %get-tuple-element.17) | data formatting | bytes 983040 | tf_op jit(solution)/shard_map/slice | solution.py:58
  249.0 2.8 %copy.76 = f32[15,8192]{1,0:T(8,128)S(1)} copy(f32[15,8192]{0,1:T(8,128)} %get-tuple-element.16) | data formatting | bytes 983040 | tf_op jit(solution)/shard_map/slice | solution.py:57
  252.9 2.8 %copy.77 = f32[15,8192]{1,0:T(8,128)S(1)} copy(f32[15,8192]{0,1:T(8,128)} %get-tuple-element.15) | data formatting | bytes 983040 | tf_op jit(solution)/shard_map/slice | solution.py:57
  256.6 2.8 %copy.78 = f32[15,8192]{1,0:T(8,128)S(1)} copy(f32[15,8192]{0,1:T(8,128)} %get-tuple-element.14) | data formatting | bytes 983040 | tf_op jit(solution)/shard_map/slice | solution.py:57
  260.5 3.9 %copy.79 = f32[15,8192]{1,0:T(8,128)} copy(f32[15,8192]{0,1:T(8,128)} %get-tuple-element.13) | data formatting | bytes 983040 | tf_op jit(solution)/shard_map/slice | solution.py:58
  266.4 3.2 %multiply_dynamic-update-slice_fusion.5 = (f32[6,60,2048]{2,1,0:T(8,128)S(1)}, f32[1,60,2048]{2,1,0:T(8,128)S(1)}, f32[1,60,2048]{2,1,0:T(8,128)S(1)}, f32[1,60,...) fusion(f32[1,60,2048]{2,1,0:T(8,128)} %mul.929, f32[1,60,2048]{2,1,0:T(8,128)} %mul.943, ...), kind=kLoop, calls=%fused_computation.33 | loop fusion | flops 2088959 | bytes 10027008
  272.1 4.2 %fusion = f32[6,35,2048]{2,1,0:T(8,128)S(1)} fusion(f32[6,35,2048]{2,1,0:T(8,128)} %negate_dynamic-update-slice_fusion, f32[6,60,2048]{2,1,0:T(8,128)S(1)} %multiply_dynamic-update-slice_fusion, f32[1,35,60]{2,0,1:T(1,128)S(1)} %copy-done.27, f32[35]{0:T(128)S(1)} %copy-done.32), kind=kOutput, calls=%fused_computation.9 | convolution fusion | flops 310089792 | bytes 6398300 | tf_op jit(solution)/shard_map/mp,qps->qms/dot_general | solution.py:79
  (131 shorter events, 54.1 us)
Async XLA Ops:
  0.0 8.7 %copy-start.30 = (f32[4,1024]{1,0:T(4,128)S(1)}, f32[4,1024]{1,0:T(4,128)}, u32[]{:S(2)}) copy-start(f32[4,1024]{1,0:T(4,128)} %param.14) | copy-start | bytes 49156
  19.7 8.0 %copy-start.23 = (s32[9216]{0:T(1024)S(1)}, s32[9216]{0:T(1024)}, u32[]{:S(2)}) copy-start(s32[9216]{0:T(1024)} %param.17) | copy-start | bytes 110596
  19.7 8.2 %copy-start.28 = (f32[1,105,35]{1,0,2:T(1,128)S(1)}, f32[1,105,35]{1,0,2:T(1,128)}, u32[]{:S(2)}) copy-start(f32[1,105,35]{1,0,2:T(1,128)} %param.19) | copy-start | bytes 44104
  19.8 9.2 %copy-start.29 = (f32[1,60,35]{1,0,2:T(1,128)S(1)}, f32[1,60,35]{1,0,2:T(1,128)}, u32[]{:S(2)}) copy-start(f32[1,60,35]{1,0,2:T(1,128)} %param.20) | copy-start | bytes 25204
  22.9 6.1 %copy-start.24 = (s32[8192]{0:T(1024)S(1)}, s32[8192]{0:T(1024)}, u32[]{:S(2)}) copy-start(s32[8192]{0:T(1024)} %param.18) | copy-start | bytes 98308
  22.9 28.9 %all-to-all-start = ((f32[235,4,512]{2,0,1:T(8,128)}), f32[235,4,512]{2,0,1:T(8,128)S(1)}, u32[]{:S(2)}, u32[]{:S(2)}) async-start(f32[235,4,512]{2,0,1:T(8,128)} %broadcast_select_fusion.1), calls=%async_computation | async-start | bytes 3932160 | tf_op jit(solution)/shard_map/all_to_all | solution.py:110
  27.9 26.5 %copy-start.31 = (f32[35]{0:T(128)}, f32[35]{0:T(128)S(1)}, u32[]{:S(2)}) copy-start(f32[35]{0:T(128)S(1)} %compare_convert_fusion) | copy-start | bytes 424
  115.5 43.9 %all-to-all-start.1 = ((f32[3,4,768,90]{2,3,0,1:T(8,128)}), f32[3,4,768,90]{2,3,0,1:T(8,128)S(1)}, u32[]{:S(2)}, u32[]{:S(2)}) async-start(f32[3,4,768,90]{2,3,0,1:T(8,128)} %broadcast_select_fusion), calls=%async_computation.1 | async-start | bytes 7077888 | tf_op jit(solution)/shard_map/all_to_all | solution.py:84
  134.2 7.2 %copy-start.9 = (f32[1,1,2048]{2,1,0:T(1,128)}, f32[1,1,2048]{2,1,0:T(1,128)S(1)}, u32[]{:S(2)}) copy-start(f32[1,1,2048]{2,1,0:T(1,128)S(1)} %get-tuple-element.28) | copy-start | bytes 24580
  134.2 7.2 %copy-start.11 = (f32[1,1,2048]{2,1,0:T(1,128)}, f32[1,1,2048]{2,1,0:T(1,128)S(1)}, u32[]{:S(2)}) copy-start(f32[1,1,2048]{2,1,0:T(1,128)S(1)} %get-tuple-element.32) | copy-start | bytes 24580
  134.2 7.2 %copy-start.13 = (f32[1,1,2048]{2,1,0:T(1,128)}, f32[1,1,2048]{2,1,0:T(1,128)S(1)}, u32[]{:S(2)}) copy-start(f32[1,1,2048]{2,1,0:T(1,128)S(1)} %get-tuple-element.33) | copy-start | bytes 24580
  134.2 7.2 %copy-start.15 = (f32[1,1,2048]{2,1,0:T(1,128)}, f32[1,1,2048]{2,1,0:T(1,128)S(1)}, u32[]{:S(2)}) copy-start(f32[1,1,2048]{2,1,0:T(1,128)S(1)} %get-tuple-element.34) | copy-start | bytes 24580
  134.2 7.2 %copy-start.17 = (f32[1,1,2048]{2,1,0:T(1,128)}, f32[1,1,2048]{2,1,0:T(1,128)S(1)}, u32[]{:S(2)}) copy-start(f32[1,1,2048]{2,1,0:T(1,128)S(1)} %get-tuple-element.29) | copy-start | bytes 24580
  134.2 7.2 %copy-start.19 = (f32[1,1,2048]{2,1,0:T(1,128)}, f32[1,1,2048]{2,1,0:T(1,128)S(1)}, u32[]{:S(2)}) copy-start(f32[1,1,2048]{2,1,0:T(1,128)S(1)} %get-tuple-element.30) | copy-start | bytes 24580
  134.2 7.2 %copy-start.21 = (f32[1,1,2048]{2,1,0:T(1,128)}, f32[1,1,2048]{2,1,0:T(1,128)S(1)}, u32[]{:S(2)}) copy-start(f32[1,1,2048]{2,1,0:T(1,128)S(1)} %get-tuple-element.31) | copy-start | bytes 24580
  161.4 16.5 %collective-permute-start.1 = (f32[4,768,90]{1,0,2:T(4,128)S(1)}, f32[4,768,90]{1,0,2:T(4,128)S(1)}, u32[]{:S(2)}, u32[]{:S(2)}) collective-permute-start(f32[4,768,90]{1,0,2:T(4,128)S(1)} %copy.71), channel_id=1, source_target_pairs={{0,1},{1,2},{2,3},{3,4},{4,5},{5,6},{6,7},{7,8},{8,9},{9,10},{10,1... | collective-permute-start | bytes 3317768 | tf_op jit(solution)/shard_map/ppermute | solution.py:15
  167.3 17.5 %collective-permute-start = (f32[4,768,90]{1,0,2:T(4,128)}, f32[4,768,90]{1,0,2:T(4,128)}, u32[]{:S(2)}, u32[]{:S(2)}) collective-permute-start(f32[4,768,90]{1,0,2:T(4,128)} %copy.69), channel_id=1, source_target_pairs={{0,31},{1,0},{2,1},{3,2},{4,3},{5,4},{6,5},{7,6},{8,7},{9,8},{10,9... | collective-permute-start | bytes 3317768 | tf_op jit(solution)/shard_map/ppermute | solution.py:15
  168.6 4.4 %copy-start.10 = (f32[1,1,2048]{2,1,0:T(1,128)S(1)}, f32[1,1,2048]{2,1,0:T(1,128)}, u32[]{:S(2)}) copy-start(f32[1,1,2048]{2,1,0:T(1,128)} %copy-done.9) | copy-start | bytes 24580
  168.6 4.4 %copy-start.18 = (f32[1,1,2048]{2,1,0:T(1,128)S(1)}, f32[1,1,2048]{2,1,0:T(1,128)}, u32[]{:S(2)}) copy-start(f32[1,1,2048]{2,1,0:T(1,128)} %copy-done.17) | copy-start | bytes 24580
  168.6 4.4 %copy-start.20 = (f32[1,1,2048]{2,1,0:T(1,128)S(1)}, f32[1,1,2048]{2,1,0:T(1,128)}, u32[]{:S(2)}) copy-start(f32[1,1,2048]{2,1,0:T(1,128)} %copy-done.19) | copy-start | bytes 24580
  168.6 4.4 %copy-start.22 = (f32[1,1,2048]{2,1,0:T(1,128)S(1)}, f32[1,1,2048]{2,1,0:T(1,128)}, u32[]{:S(2)}) copy-start(f32[1,1,2048]{2,1,0:T(1,128)} %copy-done.21) | copy-start | bytes 24580
  169.8 5.6 %copy-start.12 = (f32[1,1,2048]{2,1,0:T(1,128)S(1)}, f32[1,1,2048]{2,1,0:T(1,128)}, u32[]{:S(2)}) copy-start(f32[1,1,2048]{2,1,0:T(1,128)} %copy-done.11) | copy-start | bytes 24580
  169.8 5.6 %copy-start.14 = (f32[1,1,2048]{2,1,0:T(1,128)S(1)}, f32[1,1,2048]{2,1,0:T(1,128)}, u32[]{:S(2)}) copy-start(f32[1,1,2048]{2,1,0:T(1,128)} %copy-done.13) | copy-start | bytes 24580
  169.8 5.6 %copy-start.16 = (f32[1,1,2048]{2,1,0:T(1,128)S(1)}, f32[1,1,2048]{2,1,0:T(1,128)}, u32[]{:S(2)}) copy-start(f32[1,1,2048]{2,1,0:T(1,128)} %copy-done.15) | copy-start | bytes 24580
  175.3 10.8 %copy-start.7 = (f32[1,4,768,90]{2,3,0,1:T(8,128)S(1)}, f32[1,4,768,90]{2,3,0,1:T(8,128)}, u32[]{:S(2)}) copy-start(f32[1,4,768,90]{2,3,0,1:T(8,128)} %get-tuple-element.21) | copy-start | bytes 3317764
  190.1 4.0 %copy-start.25 = (s32[8192]{0:T(1024)S(1)}, s32[8192]{0:T(1024)}, u32[]{:S(2)}) copy-start(s32[8192]{0:T(1024)} %fusion.4) | copy-start | bytes 98308
  194.0 30.1 %copy-start.26 = (pred[8192]{0:T(1024)(128)(4,1)S(1)}, pred[8192]{0:T(1024)(128)(4,1)}, u32[]{:S(2)}) copy-start(pred[8192]{0:T(1024)(128)(4,1)} %compare_and_fusion.1) | copy-start | bytes 24580
  260.5 5.9 %copy-start.1 = (f32[6,60,2048]{2,1,0:T(8,128)S(1)}, f32[6,60,2048]{2,1,0:T(8,128)}, u32[]{:S(2)}) copy-start(f32[6,60,2048]{2,1,0:T(8,128)} %copy-done) | copy-start | bytes 8847364
  266.4 3.2 %copy-start.3 = (f32[1,60,2048]{2,1,0:T(8,128)S(1)}, f32[1,60,2048]{2,1,0:T(8,128)}, u32[]{:S(2)}) copy-start(f32[1,60,2048]{2,1,0:T(8,128)} %mul.932) | copy-start | bytes 1474564
  266.4 3.2 %copy-start.4 = (f32[1,60,2048]{2,1,0:T(8,128)S(1)}, f32[1,60,2048]{2,1,0:T(8,128)}, u32[]{:S(2)}) copy-start(f32[1,60,2048]{2,1,0:T(8,128)} %mul.939) | copy-start | bytes 1474564
  266.4 3.2 %copy-start.5 = (f32[1,60,2048]{2,1,0:T(8,128)S(1)}, f32[1,60,2048]{2,1,0:T(8,128)}, u32[]{:S(2)}) copy-start(f32[1,60,2048]{2,1,0:T(8,128)} %mul.943) | copy-start | bytes 1474564
  266.4 3.2 %copy-start.8 = (f32[1,60,2048]{2,1,0:T(8,128)S(1)}, f32[1,60,2048]{2,1,0:T(8,128)}, u32[]{:S(2)}) copy-start(f32[1,60,2048]{2,1,0:T(8,128)} %squeeze.134) | copy-start | bytes 1474564
  (5 other events, 8.9 us)
where the time goes:
time: 282 us; the launch traced here: 278 us
  local copies, waits for them, and re-layouts  164 us (58%)
  waiting for transfers between devices  43.8 us (16%)
  other arithmetic  36.3 us (13%)
  matrix products  19.4 us (7%)
  starting transfers between devices  13.1 us (5%)
    gather x2, local copies, waits for them, and re-layouts, local(): jnp.take(face_rows, send_faces, axis=0)  37.2 us
    gather x1, local copies, waits for them, and re-layouts, local(): neighbour = jnp.take(received, recv_faces, axis=0).T  30.1 us
    all_to_all x1, waiting for transfers between devices, local(): lax.all_to_all(outgoing, 'grp', split_axis=1, concat_axis=1, tiled=True)  21.5 us
    slice x4, local copies, waits for them, and re-layouts, face_flux(): jump_h = [far_split[c + 3] - own_split[c + 3] for c in range(3)]  20.7 us
    unnamed x10, other arithmetic  16.7 us
    all_to_all x1, waiting for transfers between devices, across_groups(): lax.all_to_all(outgoing, 'grp', split_axis=1, concat_axis=1, tiled=True)  15.6 us
    dot_general x1, matrix products, volume_terms(): jnp.einsum('anm,qms->qans', deriv_mats, coefficients, precision=exact_prec)  10.5 us
    slice x3, local copies, waits for them, and re-layouts, face_flux(): jump_e = [far_split[c] - own_split[c] for c in range(3)]  8.53 us
  transfers between devices with their start and end apart: 4, of which 4 were waited for; matrix products, arithmetic and copies ran while one was open for 14% of the time, Pallas kernels for 0%

commit v1 on v0

v1 whole, which is shorter than its diff:
```python
import functools

import jax
import jax.numpy as jnp
from jax import lax
from jax.experimental import pallas as pl
from jax.experimental.pallas import tpu as pltpu
from jax.sharding import PartitionSpec as P

NPM = 35
FPTS = 15
ROWS = 240
COEF = 6 * NPM
LANES = 128
ITEM = 96
NODE = 40

f32 = jnp.float32
bf16 = jnp.bfloat16
VMEM = pltpu.VMEM
SMEM = pltpu.SMEM


def halves(x):
    high = x.astype(bf16)
    return high, (x - high.astype(f32)).astype(bf16)


def dot(a, b, dims):
    return lax.dot_general(a, b, (dims, ((), ())), preferred_element_type=f32)


def dot3(a, b, dims):
    return dot(a[0], b[0], dims) + (dot(a[0], b[1], dims) + dot(a[1], b[0], dims))


def exact(a, b, dims):
    return lax.dot_general(a, b, (dims, ((), ())), preferred_element_type=f32, precision=lax.Precision.HIGHEST)


def iota(shape, dim):
    return lax.broadcasted_iota(jnp.int32, shape, dim)


def ones_where(condition):
    return jnp.where(condition, 1.0, 0.0).astype(f32)


def place_kernel(capacity, fields, metric, normals, fscale, orders, slots, out, whole, payload):
    group = pl.program_id(0)

    @pl.when(group == 0)
    def _():
        whole[0:COEF] = fields[...]
        whole[COEF : COEF + 9] = metric[...]
        whole[COEF + 9 : COEF + 21] = normals[...]
        whole[COEF + 21 : COEF + 25] = fscale[...]
        whole[COEF + 25 : ROWS] = jnp.zeros((ROWS - COEF - 25, whole.shape[1]), f32)
        high, low = halves(whole[...])
        payload[0:ROWS] = high
        payload[ROWS : 2 * ROWS] = low

    column = (orders[...] - 1 - group) * capacity + slots[...]
    column = jnp.where(orders[...] - 1 == group, column, -1)
    chosen = ones_where(iota((capacity, column.shape[1]), 0) == column).astype(bf16)
    placed = dot(payload[...], chosen, ((1,), (1,)))
    out[0] = placed[0:ROWS] + placed[ROWS : 2 * ROWS]


def place(fields, metric, normals, fscale, orders, slots, groups):
    elements = fields.shape[1]
    capacity = elements // 2
    whole = lambda rows: pl.BlockSpec((rows, elements), lambda g: (0, 0))
    return pl.pallas_call(
        functools.partial(place_kernel, capacity),
        grid=(groups,),
        in_specs=[whole(COEF), whole(9), whole(12), whole(4), whole(1), whole(1)],
        out_specs=pl.BlockSpec((1, ROWS, capacity), lambda g: (g, 0, 0)),
        out_shape=jax.ShapeDtypeStruct((groups, ROWS, capacity), f32),
        scratch_shapes=[VMEM((ROWS, elements), f32), VMEM((2 * ROWS, elements), bf16)],
        name="place",
    )(fields, metric, normals, fscale, orders.reshape(1, elements), slots.reshape(1, elements))


def prepare_kernel(group, dmat, tmat, lmat, trace_rows, trace_cols, deriv, lift):
    order = group[0]
    total = (order + 2) * (order + 3) * (order + 4) // 6
    d, t, l = dmat[0], tmat[0], lmat[0]
    t = jnp.where(iota(t.shape, 1) < total, t, 0.0)
    l = jnp.where(iota(l.shape, 0) < total, l, 0.0)
    node = iota(d.shape, 0)
    node = node - NPM * (node // NPM)
    d = jnp.where((node < total) & (iota(d.shape, 1) < total), d, 0.0)

    row, col = iota((NPM, ROWS), 0), iota((NPM, ROWS), 1)
    tile = ones_where((col - NPM * (col // NPM) == row) & (col < COEF))

    shape = (4 * ITEM, 4 * FPTS)
    row, col = iota(shape, 0), iota(shape, 1)
    face, inner = row // ITEM, row % ITEM
    pick = ones_where((inner % 16 < FPTS) & (col == (inner % 16) * 4 + face))
    spread = exact(exact(pick, t, ((1,), (0,))), tile, ((1,), (0,)))
    row, col = iota(spread.shape, 0), iota(spread.shape, 1)
    spread = jnp.where((row % ITEM) // 16 == col // NPM, spread, 0.0)
    trace_rows[0], trace_rows[1] = halves(spread)

    shape = (4 * LANES, 4 * FPTS)
    row, col = iota(shape, 0), iota(shape, 1)
    face, inner = row // LANES, row % LANES
    pick = ones_where((inner < ITEM) & (inner % 16 < FPTS) & (col == (inner % 16) * 4 + face))
    spread = exact(tile, exact(pick, t, ((1,), (0,))), ((0,), (1,)))
    row, col = iota(spread.shape, 0), iota(spread.shape, 1)
    spread = jnp.where((col % LANES) // 16 == row // NPM, spread, 0.0)
    trace_cols[0], trace_cols[1] = halves(spread)

    shape = (18 * NODE, 3 * NPM)
    row, col = iota(shape, 0), iota(shape, 1)
    inner = row % NODE
    pick = ones_where((inner < NPM) & (col == (row // (6 * NODE)) * NPM + inner))
    spread = exact(exact(pick, d, ((1,), (0,))), tile, ((1,), (0,)))
    row, col = iota(spread.shape, 0), iota(spread.shape, 1)
    spread = jnp.where((row // NODE) % 6 == col // NPM, spread, 0.0)
    deriv[0], deriv[1] = halves(spread)

    shape = (NODE, NPM)
    grow = ones_where(iota(shape, 0) == iota(shape, 1))
    shape = (4 * FPTS, 64)
    row, col = iota(shape, 0), iota(shape, 1)
    pick = ones_where((col % 16 < FPTS) & (row == (col % 16) * 4 + col // 16))
    spread = exact(grow, exact(l, pick, ((1,), (0,))), ((1,), (0,)))
    lift[0], lift[1] = halves(spread)


def prepare(group, dmat, tmat, lmat):
    return pl.pallas_call(
        prepare_kernel,
        in_specs=[pl.BlockSpec(memory_space=SMEM)] + [pl.BlockSpec(memory_space=VMEM)] * 3,
        out_specs=[pl.BlockSpec(memory_space=VMEM)] * 4,
        out_shape=[
            jax.ShapeDtypeStruct((2, 4 * ITEM, ROWS), bf16),
            jax.ShapeDtypeStruct((2, ROWS, 4 * LANES), bf16),
            jax.ShapeDtypeStruct((2, 18 * NODE, ROWS), bf16),
            jax.ShapeDtypeStruct((2, NODE, 64), bf16),
        ],
        cost_estimate=pl.CostEstimate(flops=10**9, bytes_accessed=4 * 10**6, transcendentals=0),
        name="prepare",
    )(group, dmat, tmat, lmat)


def gather_rows(index, first, source, target, start, count, unroll=32):
    def body(i, carry):
        base = pl.multiple_of(i * unroll, unroll)
        for u in range(unroll):
            row = index[first + base + u]
            target[pl.ds(start + base + u, 1), :] = source[pl.ds(row, 1), :]
        return carry

    lax.fori_loop(0, count // unroll, body, 0)


def gather_lists(index, rows, items, spill):
    lists, packed = items.shape[0], items.shape[1]
    third = packed // 3
    for h in range(lists):
        gather_rows(index, h * 4 * third, rows, items.at[h], 0, packed)
        gather_rows(index, h * 4 * third + packed, rows, spill, 0, third)
        extra = spill[...]
        lane = iota(extra.shape, 1)
        for t in range(3):
            here = pl.ds(t * third, third)
            moved = pltpu.roll(extra, ITEM - 32 * t, 1)
            items[h, here, :] = jnp.where(lane < ITEM, items[h, here, :], moved)


def traces_kernel(index, bucket, trace_cols, rows, items, spill):
    groups, _, capacity = bucket.shape
    faces = 4 * groups * capacity
    weights = (trace_cols[0], trace_cols[1])
    for g in range(groups):
        columns = halves(jnp.transpose(bucket[g]))
        traced = dot3(columns, weights, ((1,), (0,)))
        for f in range(4):
            rows[pl.ds((f * groups + g) * capacity, capacity), :] = traced[:, f * LANES : (f + 1) * LANES]
    rows[pl.ds(faces, 8), :] = jnp.zeros((8, LANES), f32)
    gather_lists(index, rows, items, spill)


def lists_kernel(index, rows, items, spill):
    gather_lists(index, rows, items, spill)


def first_lists(index, bucket, trace_cols, list_size):
    groups, _, capacity = bucket.shape
    faces = 4 * groups * capacity
    packed = list_size * 3 // 4
    return pl.pallas_call(
        traces_kernel,
        in_specs=[pl.BlockSpec(memory_space=SMEM)] + [pl.BlockSpec(memory_space=VMEM)] * 2,
        out_specs=[pl.BlockSpec(memory_space=VMEM)] * 2,
        out_shape=[
            jax.ShapeDtypeStruct((faces + 8, LANES), f32),
            jax.ShapeDtypeStruct((groups, packed, LANES), f32),
        ],
        scratch_shapes=[VMEM((packed // 3, LANES), f32)],
        name="traces",
    )(index, bucket, trace_cols)


def next_lists(index, rows, groups, list_size):
    packed = list_size * 3 // 4
    return pl.pallas_call(
        lists_kernel,
        in_specs=[pl.BlockSpec(memory_space=SMEM), pl.BlockSpec(memory_space=VMEM)],
        out_specs=pl.BlockSpec(memory_space=VMEM),
        out_shape=jax.ShapeDtypeStruct((groups, packed, LANES), f32),
        scratch_shapes=[VMEM((packed // 3, LANES), f32)],
        cost_estimate=pl.CostEstimate(flops=10**7, bytes_accessed=12 * 10**6, transcendentals=0),
        name="lists",
    )(index, rows)


def face_flux(value, normal, scale):
    e, h = value[:3], value[3:]
    half = 0.5 * scale
    normal_e = normal[0] * e[0] + normal[1] * e[1] + normal[2] * e[2]
    normal_h = normal[0] * h[0] + normal[1] * h[1] + normal[2] * h[2]

    def cross(v, c):
        return normal[(c + 1) % 3] * v[(c + 2) % 3] - normal[(c + 2) % 3] * v[(c + 1) % 3]

    flux_e = [half * (cross(h, c) + e[c] - normal[c] * normal_e) for c in range(3)]
    flux_h = [half * (h[c] - cross(e, c) - normal[c] * normal_h) for c in range(3)]
    return flux_e + flux_h


def own_kernel(bucket, deriv, trace_rows, lift, part, geometry, flux):
    cols = halves(bucket[0])
    derived = dot3((deriv[0], deriv[1]), cols, ((1,), (0,)))
    row = lambda r: bucket[0, r : r + 1, :]
    metric = [[row(COEF + 3 * a + x) for x in range(3)] for a in range(3)]

    def along(component, x):
        take = lambda a: derived[(a * 6 + component) * NODE : (a * 6 + component + 1) * NODE]
        return metric[0][x] * take(0) + metric[1][x] * take(1) + metric[2][x] * take(2)

    volume = []
    for sign, first in ((1, 3), (-1, 0)):
        for c in range(3):
            y, z = (c + 1) % 3, (c + 2) % 3
            curl = along(first + z, y) - along(first + y, z)
            volume.append(curl if sign > 0 else -curl)
    geometry[...] = bucket[0, COEF + 9 : COEF + 25, :]
    own = dot3((trace_rows[0], trace_rows[1]), cols, ((1,), (0,)))
    for f in range(4):
        value = [own[f * ITEM + 16 * c : f * ITEM + 16 * (c + 1)] for c in range(6)]
        normal = [geometry[4 * c + f : 4 * c + f + 1, :] for c in range(3)]
        for c, part_of in enumerate(face_flux(value, normal, geometry[12 + f : 13 + f, :])):
            flux[c, 16 * f : 16 * (f + 1)] = part_of
    lifts = (lift[0], lift[1])
    for c in range(6):
        part[c * NODE : (c + 1) * NODE] = volume[c] - dot3(lifts, halves(flux[c]), ((1,), (0,)))


def own_part(bucket, deriv, trace_rows, lift):
    groups, _, capacity = bucket.shape
    fixed = lambda x: pl.BlockSpec(x.shape, lambda g: (0,) * x.ndim)
    return pl.pallas_call(
        own_kernel,
        grid=(groups,),
        in_specs=[pl.BlockSpec((1, ROWS, capacity), lambda g: (g, 0, 0)), fixed(deriv), fixed(trace_rows), fixed(lift)],
        out_specs=[pl.BlockSpec((6 * NODE, capacity), lambda g: (0, g)), pl.BlockSpec((16, capacity), lambda g: (0, g))],
        out_shape=[
            jax.ShapeDtypeStruct((6 * NODE, groups * capacity), f32),
            jax.ShapeDtypeStruct((16, groups * capacity), f32),
        ],
        scratch_shapes=[VMEM((6, 64, capacity), f32)],
        cost_estimate=pl.CostEstimate(flops=5 * 10**9, bytes_accessed=8 * 10**6, transcendentals=0),
        name="own_part",
    )(bucket, deriv, trace_rows, lift)


def finish_kernel(width, index, low, mid, high, part, geometry, lift, out, rows, near, flux, sems):
    step = pl.program_id(0)
    groups, packed, _ = low.shape
    third = packed // 3
    lists = 3 * groups
    slots = pl.num_programs(0) * width

    @pl.when(step == 0)
    def _():
        copies = []
        for j, source in enumerate((low, mid, high)):
            for g in range(groups):
                target = rows.at[pl.ds((j * groups + g) * packed, packed), :]
                copies.append(pltpu.make_async_copy(source.at[g], target, sems.at[j, g]))
        for copy in copies:
            copy.start()
        rows[pl.ds(lists * (packed + third), 8), :] = jnp.zeros((8, LANES), f32)
        lane = iota((third, LANES), 1)
        for n, copy in enumerate(copies):
            copy.wait()
            piece = [
                pltpu.roll(rows[pl.ds(n * packed + t * third, third), :], 32 * (t + 1), 1) for t in range(3)
            ]
            rows[pl.ds(lists * packed + n * third, third), :] = jnp.where(
                lane < 32, piece[0], jnp.where(lane < 64, piece[1], piece[2])
            )

    for f in range(4):
        gather_rows(index, f * slots + step * width, rows, near.at[f], 0, width)
    for f in range(4):
        turned = jnp.transpose(near[f])
        value = [turned[16 * c : 16 * (c + 1)] for c in range(6)]
        normal = [geometry[4 * c + f : 4 * c + f + 1, :] for c in range(3)]
        for c, part_of in enumerate(face_flux(value, normal, geometry[12 + f : 13 + f, :])):
            flux[c, 16 * f : 16 * (f + 1)] = part_of
    lifts = (lift[0], lift[1])
    for c in range(6):
        total = part[c * NODE : (c + 1) * NODE] + dot3(lifts, halves(flux[c]), ((1,), (0,)))
        out[c * NPM : (c + 1) * NPM] = total[:NPM]


def finish(index, low, mid, high, part, geometry, lift, width=256):
    groups, packed, _ = low.shape
    slots = part.shape[1]
    third = packed // 3
    block = lambda rows: pl.BlockSpec((rows, width), lambda s: (0, s))
    return pl.pallas_call(
        functools.partial(finish_kernel, width),
        grid=(slots // width,),
        in_specs=[pl.BlockSpec(memory_space=SMEM)]
        + [pl.BlockSpec(memory_space=pl.ANY)] * 3
        + [block(6 * NODE), block(16), pl.BlockSpec(lift.shape, lambda s: (0, 0, 0))],
        out_specs=block(COEF),
        out_shape=jax.ShapeDtypeStruct((COEF, slots), f32),
        scratch_shapes=[
            VMEM((3 * groups * (packed + third) + 8, LANES), f32),
            VMEM((4, width, LANES), f32),
            VMEM((6, 64, width), f32),
            pltpu.SemaphoreType.DMA((3, groups)),
        ],
        name="finish",
    )(index, low, mid, high, part, geometry, lift)


def exchange(x):
    return lax.all_to_all(x, "grp", split_axis=0, concat_axis=0, tiled=True)


def shifted(x, by):
    size = lax.axis_size("dom")
    return lax.ppermute(x, "dom", [(i, (i + by) % size) for i in range(size)])


def local(fields, metric, normals, fscale, orders, slots, send_faces, recv_faces, dmat, tmat, lmat):
    groups = lax.axis_size("grp")
    list_total = send_faces.shape[0]
    list_size = list_total // (3 * groups)
    packed = list_size * 3 // 4
    third = packed // 3
    sends = send_faces.reshape(3, groups * list_size)
    entry, place_in = recv_faces // list_size, recv_faces % list_size
    where = jnp.where(
        place_in < packed, entry * packed + place_in, 3 * groups * packed + entry * third + place_in - packed
    )
    where = jnp.where(recv_faces < list_total, where, list_total)

    bucket = exchange(place(fields, metric, normals, fscale, orders, slots, groups))
    group = lax.axis_index("grp").astype(jnp.int32).reshape(1)
    trace_rows, trace_cols, deriv, lift = prepare(group, dmat, tmat, lmat)
    rows, low = first_lists(sends[0], bucket, trace_cols, list_size)
    low = shifted(exchange(low), -1)
    high = shifted(exchange(next_lists(sends[2], rows, groups, list_size)), 1)
    mid = exchange(next_lists(sends[1], rows, groups, list_size))
    part, geometry = own_part(bucket, deriv, trace_rows, lift)
    return finish(where, low, mid, high, part, geometry, lift)


def solution(mesh):
    in_specs = (
        P(None, ("grp", "dom")),
        P(None, ("grp", "dom")),
        P(None, ("grp", "dom")),
        P(None, ("grp", "dom")),
        P(("grp", "dom")),
        P(("grp", "dom")),
        P(("grp", "dom")),
        P(("grp", "dom")),
        P("grp", None, None),
        P("grp", None, None),
        P("grp", None, None),
    )
    out_specs = P(None, ("grp", "dom"))
    return jax.shard_map(local, mesh=mesh, in_specs=in_specs, out_specs=out_specs, check_vma=False)
```

time: 282 us -> 138 us (0.49)
  local copies, waits for them, and re-layouts: 164 us -> 5.75 us
  Pallas kernels: 0 us -> 58.2 us
  other arithmetic: 36.3 us -> 1.41 us
  matrix products: 19.4 us -> 0 us
  blocking collectives: 0 us -> 19.1 us
  waiting for transfers between devices: 43.8 us -> 32.3 us
  starting transfers between devices: 13.1 us -> 19.8 us
    gather x5 -> x0, local copies, waits for them, and re-layouts: 75.8 us -> none  [the longest x2 37.2 us: local(): jnp.take(face_rows, send_faces, axis=0)]
    pallas_call x0 -> x7, Pallas kernels: none -> 58.2 us  [the longest x1 16.6 us: finish(): pl.pallas_call(functools.partial(finish_kernel, width), grid=(slots // wi...]
    slice x12 -> x1, local copies, waits for them, and re-layouts: 33.1 us -> 0.61 us  [local(): high = shifted(exchange(next_lists(sends[2], rows, groups, list_size)), 1)]
    dot_general x3 -> x0, matrix products: 19.4 us -> none  [the longest x1 10.5 us: volume_terms(): jnp.einsum('anm,qms->qans', deriv_mats, coefficients, precision=exact_prec)]
    all_to_all x0 -> x1, blocking collectives: none -> 19.1 us  [exchange(): return lax.all_to_all(x, 'grp', split_axis=0, concat_axis=0, tiled=True)]
    unnamed x10 -> x0, other arithmetic: 16.7 us -> none
    reshape x6 -> x0, local copies, waits for them, and re-layouts: 16.2 us -> none  [the longest x2 8.15 us: local(): jnp.einsum('pm,qms->qps', trace_mat, coefficients, precision=exact_prec)]
    select_n x4 -> x1, other arithmetic: 12.3 us -> 1.41 us  [local(): where = jnp.where(recv_faces < list_total, where, list_total)]
  transfers between devices with their start and end apart: 4 -> 5, of which waited for: 4 -> 3; matrix products, arithmetic and copies ran while one was open for 14% -> 3% of each run, Pallas kernels for 0% -> 15%
where the time goes in v1:
time: 138 us; the launch traced here: 137 us
  Pallas kernels  58.2 us (42%)
  waiting for transfers between devices  32.3 us (23%)
  starting transfers between devices  19.8 us (14%)
  blocking collectives  19.1 us (14%)
  local copies, waits for them, and re-layouts  5.75 us (4%)
  other arithmetic  1.41 us (1%)
    all_to_all x3, waiting for transfers between devices, exchange(): return lax.all_to_all(x, 'grp', split_axis=0, concat_axis=0, tiled=True)  32.3 us
    all_to_all x1, blocking collectives, exchange(): return lax.all_to_all(x, 'grp', split_axis=0, concat_axis=0, tiled=True)  19.1 us
    pallas_call x1, Pallas kernels, finish(): pl.pallas_call(functools.partial(finish_kernel, width), grid=(slots // wi...  16.6 us
    pallas_call x2, Pallas kernels, next_lists(): pl.pallas_call(lists_kernel, in_specs=[pl.BlockSpec(memory_space=SMEM), p...  13.2 us
    all_to_all x3, starting transfers between devices, exchange(): return lax.all_to_all(x, 'grp', split_axis=0, concat_axis=0, tiled=True)  12.1 us
    pallas_call x1, Pallas kernels, first_lists(): pl.pallas_call(traces_kernel, in_specs=[pl.BlockSpec(memory_space=SMEM)]...  9.17 us
    pallas_call x1, Pallas kernels, own_part(): pl.pallas_call(own_kernel, grid=(groups,), in_specs=[pl.BlockSpec((1, ROW...  8.73 us
    ppermute x2, starting transfers between devices, shifted(): return lax.ppermute(x, 'dom', [(i, (i + by) % size) for i in range(size)])  7.73 us
  transfers between devices with their start and end apart: 5, of which 3 were waited for; matrix products, arithmetic and copies ran while one was open for 3% of the time, Pallas kernels for 15%

profile of v1, /device:TPU:39, one launch (start us, length us, event | category | flops | bytes accessed | tf_op | source)
XLA Modules:
  0.0 136.7 jit_solution(12277010464154237206)
XLA Ops:
  0.0 5.2 %place.1 = f32[4,240,512]{2,1,0:T(8,128)} custom-call(f32[210,1024]{1,0:T(8,128)} %fields.1, f32[9,1024]{1,0:T(8,128)} %metric.1, f32[12,1024]{1,0:T(8,128)} %normals.1, f32[4,1024]{1,0:T(4,128)} %fscale.1, s32[1,1024]{1,0:T(1,128)} %bitcast.3, s32[1,1024]{1,0:T(1,128)} %bitcast.4), custom_call_target="tpu_custom_call" | custom-call | tf_op jit(solution)/shard_map/place/pallas_call | solution.py:74
  5.2 4.3 %all-to-all-start = ((f32[4,240,512]{2,1,0:T(8,128)}), f32[4,240,512]{2,1,0:T(8,128)S(1)}, u32[]{:S(2)}, u32[]{:S(2)}) async-start(f32[4,240,512]{2,1,0:T(8,128)} %place.1), calls=%async_computation | async-start | bytes 3932160 | tf_op jit(solution)/shard_map/all_to_all | solution.py:347
  9.5 0.0 copy-done.5
  9.5 0.7 copy.12.dmat
  10.3 0.0 copy-done.6
  10.3 0.7 copy.13.tmat
  11.0 0.0 copy-done.7
  11.0 0.6 copy.14.lmat
  11.6 5.3 %prepare.1 = (bf16[2,384,240]{2,1,0:T(8,128)(2,1)}, bf16[2,240,512]{2,1,0:T(8,128)(2,1)}, bf16[2,720,240]{2,1,0:T(8,128)(2,1)}, bf16[2,40,64]{2,1,0:T(8,128)(2,1)}) custom-call(s32[1]{0:T(128)} %bitcast.2.group, f32[1,105,35]{2,1,0:T(8,128)} %copy.12.dmat, f32[1,60,35]{2,1,0:T(8,128)} %copy.13.tmat, f32[1,35,60]{2,1,0:T(8,128)} %copy.14.lmat), custom_call_target="tpu_custom_call" | custom-call | flops 1000000000 | bytes 4000000 | tf_op jit(solution)/shard_map/prepare/pallas_call | solution.py:135
  16.9 0.0 copy-done.4
  16.9 0.6 fusion.1
  17.5 16.1 %all-to-all-done.bucket = f32[4,240,512]{2,1,0:T(8,128)S(1)} async-done(((f32[4,240,512]{2,1,0:T(8,128)}), f32[4,240,512]{2,1,0:T(8,128)S(1)}, u32[]{:S(2)}, u32[]{:S(2)}) %all-to-all-start) | async-done | bytes 1966112 | tf_op jit(solution)/shard_map/all_to_all | solution.py:347
  33.6 1.3 copy-done
  34.9 9.2 %traces.1 = (f32[8200,128]{1,0:T(8,128)}, f32[4,576,128]{2,1,0:T(8,128)}) custom-call(s32[3072]{0:T(1024)} %get-tuple-element.22.index, f32[4,240,512]{2,1,0:T(8,128)} %copy-done, bf16[2,240,512]{2,1,0:T(8,128)(2,1)} %get-tuple-element.13.trace_cols), custom_call_target="tpu_custom_call" | custom-call | tf_op jit(solution)/shard_map/traces/pallas_call | solution.py:196
  44.1 6.6 %lists.3 = f32[4,576,128]{2,1,0:T(8,128)} custom-call(s32[3072]{0:T(1024)} %get-tuple-element.21.index, f32[8200,128]{1,0:T(8,128)} %get-tuple-element.15.rows), custom_call_target="tpu_custom_call" | custom-call | flops 10000000 | bytes 12000000 | tf_op jit(solution)/shard_map/lists/pallas_call | solution.py:211
  50.7 19.1 %all_to_all.20 = f32[4,576,128]{2,1,0:T(8,128)} all-to-all(f32[4,576,128]{2,1,0:T(8,128)} %lists.3), channel_id=1, replica_groups=mesh['grp'=4,'dom'=32] {'grp'}, dimensions={0} | all-to-all | bytes 2359296 | tf_op jit(solution)/shard_map/all_to_all | solution.py:347
  69.8 4.3 %all-to-all-start.1 = ((f32[4,576,128]{2,1,0:T(8,128)}), f32[4,576,128]{2,1,0:T(8,128)}, u32[]{:S(2)}, u32[]{:S(2)}) async-start(f32[4,576,128]{2,1,0:T(8,128)} %get-tuple-element.14), calls=%async_computation.1 | async-start | bytes 2359296 | tf_op jit(solution)/shard_map/all_to_all | solution.py:347
  74.0 4.2 %collective-permute-start.1 = (f32[4,576,128]{2,1,0:T(8,128)}, f32[4,576,128]{2,1,0:T(8,128)S(1)}, u32[]{:S(2)}, u32[]{:S(2)}) collective-permute-start(f32[4,576,128]{2,1,0:T(8,128)} %all_to_all.20), channel_id=1, source_target_pairs={{0,1},{1,2},{2,3},{3,4},{4,5},{5,6},{6,7},{7,8},{8,9},{9,10},{10,1... | collective-permute-start | bytes 3538952 | tf_op jit(solution)/shard_map/ppermute | solution.py:352
  78.2 9.8 %all-to-all-done.1 = f32[4,576,128]{2,1,0:T(8,128)} async-done(((f32[4,576,128]{2,1,0:T(8,128)}), f32[4,576,128]{2,1,0:T(8,128)}, u32[]{:S(2)}, u32[]{:S(2)}) %all-to-all-start.1) | async-done | bytes 1179680 | tf_op jit(solution)/shard_map/all_to_all | solution.py:347
  88.0 3.5 %collective-permute-start = (f32[4,576,128]{2,1,0:T(8,128)}, f32[4,576,128]{2,1,0:T(8,128)S(1)}, u32[]{:S(2)}, u32[]{:S(2)}) collective-permute-start(f32[4,576,128]{2,1,0:T(8,128)} %all-to-all-done.1), channel_id=1, source_target_pairs={{0,31},{1,0},{2,1},{3,2},{4,3},{5,4},{6,5},{7,6},{8,7},{9,8},{10,9... | collective-permute-start | bytes 3538952 | tf_op jit(solution)/shard_map/ppermute | solution.py:352
  91.6 6.6 %lists.2 = f32[4,576,128]{2,1,0:T(8,128)} custom-call(s32[3072]{0:T(1024)} %get-tuple-element.23.index, f32[8200,128]{1,0:T(8,128)} %get-tuple-element.15.rows), custom_call_target="tpu_custom_call" | custom-call | flops 10000000 | bytes 12000000 | tf_op jit(solution)/shard_map/lists/pallas_call | solution.py:211
  98.2 3.5 %all-to-all-start.2 = ((f32[4,576,128]{2,1,0:T(8,128)}), f32[4,576,128]{2,1,0:T(8,128)S(1)}, u32[]{:S(2)}, u32[]{:S(2)}) async-start(f32[4,576,128]{2,1,0:T(8,128)} %lists.2), calls=%async_computation.2 | async-start | bytes 2359296 | tf_op jit(solution)/shard_map/all_to_all | solution.py:347
  101.7 1.4 %select_select_fusion.index = s32[8192]{0:T(1024)} fusion(s32[8192]{0:T(1024)} %param.18), kind=kLoop, calls=%fused_computation.2 | loop fusion | flops 180224 | bytes 65536 | tf_op jit(solution)/shard_map/jit(_where)/select_n | solution.py:366
  103.1 8.7 %own_part.1 = (f32[240,2048]{1,0:T(8,128)}, f32[16,2048]{1,0:T(8,128)}) custom-call(f32[4,240,512]{2,1,0:T(8,128)} %copy-done, bf16[2,720,240]{2,1,0:T(8,128)(2,1)} %get-tuple-element.16.deriv, bf16[2,384,240]{2,1,0:T(8,128)(2,1)} %get-tuple-element.17.trace_rows, bf16[2,40,64]{2,1,0:T(8,128)(2,1)} %get-tuple-element.18.lift), custom_call_target="tpu_custom_call" | custom-call | flops 5000000000 | bytes 8000000 | tf_op jit(solution)/shard_map/own_part/pallas_call | solution.py:267
  111.8 6.4 %all-to-all-done.2.mid = f32[4,576,128]{2,1,0:T(8,128)S(1)} async-done(((f32[4,576,128]{2,1,0:T(8,128)}), f32[4,576,128]{2,1,0:T(8,128)S(1)}, u32[]{:S(2)}, u32[]{:S(2)}) %all-to-all-start.2) | async-done | bytes 1179680 | tf_op jit(solution)/shard_map/all_to_all | solution.py:347
  118.3 0.0 collective-permute-done.1.high
  118.3 0.0 collective-permute-done.low
  118.3 0.0 copy-start.3
  118.3 1.0 copy-done.1
  119.3 0.4 copy-done.2
  119.6 0.5 copy-done.3
  120.1 16.6 %finish.1 = f32[210,2048]{1,0:T(8,128)} custom-call(s32[8192]{0:T(1024)} %select_select_fusion.index, f32[4,576,128]{2,1,0:T(8,128)} %copy-done.3, f32[4,576,128]{2,1,0:T(8,128)} %copy-done.1, f32[4,576,128]{2,1,0:T(8,128)} %copy-done.2, f32[240,2048]{1,0:T(8,128)} %get-tuple-element.19.part, f32[16,2048]{1,0:T(8,128)} %get-tuple-element.20.geometry, ...), custom_call_target="tpu_custom_call" | custom-call | tf_op jit(solution)/shard_map/finish/pallas_call | solution.py:328
  (7 shorter events, 0.0 us)
Async XLA Ops:
  5.2 4.3 %copy-start.5 = (f32[1,105,35]{1,0,2:T(1,128)S(1)}, f32[1,105,35]{1,0,2:T(1,128)}, u32[]{:S(2)}) copy-start(f32[1,105,35]{1,0,2:T(1,128)} %param.19) | copy-start | bytes 44104
  5.2 5.1 %copy-start.6 = (f32[1,60,35]{1,0,2:T(1,128)S(1)}, f32[1,60,35]{1,0,2:T(1,128)}, u32[]{:S(2)}) copy-start(f32[1,60,35]{1,0,2:T(1,128)} %param.20) | copy-start | bytes 25204
  5.2 5.8 %copy-start.7 = (f32[1,35,60]{2,0,1:T(1,128)S(1)}, f32[1,35,60]{2,0,1:T(1,128)}, u32[]{:S(2)}) copy-start(f32[1,35,60]{2,0,1:T(1,128)} %param.21) | copy-start | bytes 25204
  5.2 28.4 %all-to-all-start = ((f32[4,240,512]{2,1,0:T(8,128)}), f32[4,240,512]{2,1,0:T(8,128)S(1)}, u32[]{:S(2)}, u32[]{:S(2)}) async-start(f32[4,240,512]{2,1,0:T(8,128)} %place.1), calls=%async_computation | async-start | bytes 3932160 | tf_op jit(solution)/shard_map/all_to_all | solution.py:347
  11.6 5.3 %copy-start.4 = (s32[9216]{0:T(1024)S(1)}, s32[9216]{0:T(1024)}, u32[]{:S(2)}) copy-start(s32[9216]{0:T(1024)} %param.17) | copy-start | bytes 110596
  33.6 1.3 copy-start
  69.8 18.3 %all-to-all-start.1 = ((f32[4,576,128]{2,1,0:T(8,128)}), f32[4,576,128]{2,1,0:T(8,128)}, u32[]{:S(2)}, u32[]{:S(2)}) async-start(f32[4,576,128]{2,1,0:T(8,128)} %get-tuple-element.14), calls=%async_computation.1 | async-start | bytes 2359296 | tf_op jit(solution)/shard_map/all_to_all | solution.py:347
  74.0 44.2 %collective-permute-start.1 = (f32[4,576,128]{2,1,0:T(8,128)}, f32[4,576,128]{2,1,0:T(8,128)S(1)}, u32[]{:S(2)}, u32[]{:S(2)}) collective-permute-start(f32[4,576,128]{2,1,0:T(8,128)} %all_to_all.20), channel_id=1, source_target_pairs={{0,1},{1,2},{2,3},{3,4},{4,5},{5,6},{6,7},{7,8},{8,9},{9,10},{10,1... | collective-permute-start | bytes 3538952 | tf_op jit(solution)/shard_map/ppermute | solution.py:352
  88.0 30.2 %collective-permute-start = (f32[4,576,128]{2,1,0:T(8,128)}, f32[4,576,128]{2,1,0:T(8,128)S(1)}, u32[]{:S(2)}, u32[]{:S(2)}) collective-permute-start(f32[4,576,128]{2,1,0:T(8,128)} %all-to-all-done.1), channel_id=1, source_target_pairs={{0,31},{1,0},{2,1},{3,2},{4,3},{5,4},{6,5},{7,6},{8,7},{9,8},{10,9... | collective-permute-start | bytes 3538952 | tf_op jit(solution)/shard_map/ppermute | solution.py:352
  98.2 20.1 %all-to-all-start.2 = ((f32[4,576,128]{2,1,0:T(8,128)}), f32[4,576,128]{2,1,0:T(8,128)S(1)}, u32[]{:S(2)}, u32[]{:S(2)}) async-start(f32[4,576,128]{2,1,0:T(8,128)} %lists.2), calls=%async_computation.2 | async-start | bytes 2359296 | tf_op jit(solution)/shard_map/all_to_all | solution.py:347
  118.3 1.0 copy-start.1
  118.3 1.4 %copy-start.2 = (f32[4,576,128]{2,1,0:T(8,128)}, f32[4,576,128]{2,1,0:T(8,128)S(1)}, u32[]{:S(2)}) copy-start(f32[4,576,128]{2,1,0:T(8,128)S(1)} %collective-permute-done.1.high) | copy-start | bytes 3538948
  118.3 1.8 %copy-start.3 = (f32[4,576,128]{2,1,0:T(8,128)}, f32[4,576,128]{2,1,0:T(8,128)S(1)}, u32[]{:S(2)}) copy-start(f32[4,576,128]{2,1,0:T(8,128)S(1)} %collective-permute-done.low) | copy-start | bytes 3538948
